TPU v7x, 32 devices: a whole 2x2x4 slice. The times are simulated.
32 devices in a mesh: domain: 2 (over x), fsdp: 16 (over z, y, core).
Axes of the slice: x: 2, y: 2, z: 4, core: 2. Of those that a mesh axis runs over, the one named last changes fastest.
Arguments:
- gradients: bfloat16 [2, 4, 4096, 512], P('domain', None, 'fsdp')
- row_counts: int32 [4], replicated, may hold values from 2048 to 4096, as said below
- domain_ids: int32 [2], replicated, may hold values from 0 to 7
- domain_weights: float32 [8], replicated, may hold values from 0.2 to 2
Outputs:
- updates: float32 [4, 4096, 512], P('domain', 'fsdp')
- new_weights: float32 [8], replicated
Inputs may be any that keep to these rules, and one draw needn't show every extreme that they name: `row_counts`: each matrix has 4096 or 2048 rows, and both counts occur.
All inputs are finite; a program needn't handle non-finite values.
Results may differ from a plain program's by a relative error of at most 0.0071.
Values may be sent and summed in bfloat16 or wider, within the bound.
No kernel may reach another device: no remote copies, remote signals or barrier semaphores. Data moves between devices by JAX's collectives and lax.ppermute only.
A program may use at most 64 MiB of HBM per device.

v0:
```python
import math
import jax
import jax.numpy as jnp
from jax import lax
from jax.sharding import PartitionSpec as P

NS_ITERS = 3
OWNERS = 8
COEF_A = 3.4445
COEF_B = -4.775
COEF_C = 2.0315
MUON_SCALE = 0.2
ETA = 4.0


def partner(shard, axis, stride):
    return lax.ppermute(shard, axis, [(i, i ^ 1 << stride) for i in range(lax.axis_size(axis))])


def group_mixing(domain_ids, domain_weights, kind_count):
    weight_share = domain_weights / jnp.sum(domain_weights)
    onehot = (domain_ids[:, None] == jnp.arange(kind_count, dtype=jnp.int32)[None, :]).astype(
        jnp.float32
    )
    counts = jnp.sum(onehot, axis=0)
    per_member = weight_share / jnp.maximum(counts, 1.0)
    group_mix = jnp.sum(onehot * per_member[None, :], axis=1)
    return (weight_share, onehot, counts, group_mix)


def summed_gram(iterate):
    gram_total = lax.dot_general(
        iterate, iterate, (((0,), (0,)), ((), ())), preferred_element_type=jnp.float32
    )
    for bit_pos in range(OWNERS.bit_length() - 1):
        gram_total = gram_total + partner(gram_total, "fsdp", bit_pos)
    return gram_total


def newton_steps(iterate):
    for repeat in range(NS_ITERS):
        gram_full = lax.optimization_barrier(summed_gram(iterate).astype(jnp.bfloat16))
        square = jnp.dot(gram_full, gram_full, preferred_element_type=jnp.float32)
        poly_term = (COEF_B * gram_full.astype(jnp.float32) + COEF_C * square).astype(jnp.bfloat16)
        iterate = lax.optimization_barrier(
            (
                COEF_A * iterate.astype(jnp.float32)
                + jnp.dot(iterate, poly_term, preferred_element_type=jnp.float32)
            ).astype(jnp.bfloat16)
        )
    return iterate


def share_scores(aligned, squares, norm_slots):
    return lax.psum((aligned, squares, norm_slots), ("domain", "fsdp"))


def body(gradients, row_counts, domain_ids, domain_weights):
    groups = lax.axis_size("domain")
    shards = lax.axis_size("fsdp")
    matrices = row_counts.shape[0]
    rows_src = gradients.shape[2]
    columns = gradients.shape[3]
    per_domain = matrices // groups
    sub_rows = rows_src // OWNERS
    own_rows = shards * sub_rows
    full_rows = rows_src * shards
    domain_pos = lax.axis_index("domain")
    shard_pos = lax.axis_index("fsdp")
    weight_share, onehot, counts, group_mix = group_mixing(
        domain_ids, domain_weights, domain_weights.shape[0]
    )
    blocks = lax.all_to_all(
        gradients.reshape(1, groups, per_domain, rows_src, columns),
        "domain",
        split_axis=1,
        concat_axis=0,
        tiled=True,
    )
    blocks = blocks.reshape(groups, per_domain, rows_src, columns)
    global_rows = shard_pos * rows_src + jnp.arange(rows_src, dtype=jnp.int32)
    limits = lax.dynamic_slice_in_dim(row_counts, domain_pos * per_domain, per_domain, 0)
    row_mask = (global_rows[None, :] < limits[:, None])[None, :, :, None]
    masked = jnp.where(row_mask, blocks.astype(jnp.float32), jnp.zeros((), jnp.float32))
    combined = jnp.sum(group_mix[:, None, None, None] * masked, axis=0)
    aligned = jnp.sum(masked * combined[None], axis=(1, 2, 3))
    squares = jnp.sum(masked * masked, axis=(1, 2, 3))
    block_squares = jnp.sum(combined * combined, axis=(1, 2))
    norm_slots = lax.dynamic_update_slice_in_dim(
        jnp.zeros((matrices,), jnp.float32), block_squares, domain_pos * per_domain, 0
    )
    aligned, squares, norm_slots = share_scores(aligned, squares, norm_slots)
    frob_norm = (
        jnp.sqrt(lax.dynamic_slice_in_dim(norm_slots, domain_pos * per_domain, per_domain, 0))
        + 1e-07
    )
    scaled = (combined / frob_norm[:, None, None]).astype(jnp.bfloat16)
    scaled = scaled.reshape(shards, 1, sub_rows, columns)
    start_rows = lax.all_to_all(scaled, "fsdp", split_axis=0, concat_axis=1, tiled=True)
    start_rows = lax.optimization_barrier(start_rows.reshape(own_rows, columns))
    finished = newton_steps(start_rows)
    returned = lax.all_to_all(
        finished.reshape(1, shards, sub_rows, columns),
        "fsdp",
        split_axis=1,
        concat_axis=0,
        tiled=True,
    )
    returned = returned.reshape(per_domain, rows_src, columns)
    updates = returned.astype(jnp.float32) * (MUON_SCALE * math.sqrt(full_rows))
    total_sq = jnp.sum(norm_slots)
    cosine = aligned / (jnp.sqrt(squares) * jnp.sqrt(total_sq) + 1e-06)
    score = jnp.sum(onehot * cosine[:, None], axis=0) / jnp.maximum(counts, 1.0)
    raised = weight_share * jnp.exp(ETA * score)
    return (updates, raised / jnp.sum(raised))


def solution(mesh):
    placed = (P("domain", None, "fsdp", None), P(), P(), P())
    return jax.shard_map(
        body,
        mesh=mesh,
        in_specs=placed,
        out_specs=(P("domain", "fsdp", None), P()),
        check_vma=False,
    )
```

profile of v0, /device:TPU:0, one launch (start us, length us, event | category | flops | bytes accessed | tf_op | source)
XLA Modules:
  0.0 265.7 jit_solution(6877497156156330844)
XLA Ops:
  0.7 4.4 %all-to-all-start = ((bf16[1,2,2,256,512]{4,3,2,0,1:T(8,128)(2,1)}), bf16[1,2,2,256,512]{4,3,2,0,1:T(8,128)(2,1)S(1)}, u32[]{:S(2)}, u32[]{:S(2)}) async-start(bf16[1,2,2,256,512]{4,3,2,0,1:T(8,128)(2,1)} %bitcast.31), calls=%async_computation | async-start | bytes 2097152 | tf_op jit(solution)/shard_map/all_to_all | solution.py:73
  5.1 0.6 reduce_sum.92
  5.8 0.7 multiply_divide_fusion
  6.7 12.7 %all-to-all-done = bf16[1,2,2,256,512]{4,3,2,0,1:T(8,128)(2,1)S(1)} async-done(((bf16[1,2,2,256,512]{4,3,2,0,1:T(8,128)(2,1)}), bf16[1,2,2,256,512]{4,3,2,0,1:T(8,128)(2,1)S(1)}, u32[]{:S(2)}, u32[]{:S(2)}) %all-to-all-start) | async-done | bytes 1048608 | tf_op jit(solution)/shard_map/all_to_all | solution.py:73
  20.2 0.7 fusion.5
  20.9 39.8 %all-reduce = (f32[4]{0:T(128)S(1)}, f32[2]{0:T(128)S(1)}, f32[2]{0:T(128)S(1)}) all-reduce(f32[4]{0:T(128)S(1)} %dynamic_update_slice.3, f32[2]{0:T(128)S(1)} %get-tuple-element.3, f32[2]{0:T(128)S(1)} %get-tuple-element.2), channel_id=1, replica_groups=mesh['domain'=2,'fsdp'=16] {'domain','fsdp'}, use_global_device_ids=true, to_apply=%region_5.6 | all-reduce | flops 8 | bytes 64 | tf_op jit(solution)/shard_map/psum | solution.py:55
  60.7 0.6 reduce_sum.100
  62.4 19.5 %all_to_all.12 = bf16[16,1,32,512]{3,2,1,0:T(8,128)(2,1)S(1)} all-to-all(bf16[16,1,32,512]{3,2,1,0:T(8,128)(2,1)S(1)} %divide_convert_fusion), channel_id=1, replica_groups=mesh['domain'=2,'fsdp'=16] {'fsdp'}, dimensions={0} | all-to-all | bytes 1048576 | tf_op jit(solution)/shard_map/all_to_all | solution.py:99
  81.9 0.5 fusion.22
  82.6 2.5 collective-permute-done
  85.3 1.1 collective-permute-start.1
  86.4 24.2 %collective-permute-done.1 = f32[512,512]{1,0:T(8,128)S(1)} collective-permute-done((f32[512,512]{1,0:T(8,128)S(1)}, f32[512,512]{1,0:T(8,128)S(1)}, u32[]{:S(2)}, u32[]{:S(2)}) %collective-permute-start.1) | collective-permute-done | bytes 1048608 | tf_op jit(solution)/shard_map/ppermute | solution.py:17
  110.8 1.8 collective-permute-start.2
  112.6 22.8 %collective-permute-done.2 = f32[512,512]{1,0:T(8,128)S(1)} collective-permute-done((f32[512,512]{1,0:T(8,128)S(1)}, f32[512,512]{1,0:T(8,128)S(1)}, u32[]{:S(2)}, u32[]{:S(2)}) %collective-permute-start.2) | collective-permute-done | bytes 1048608 | tf_op jit(solution)/shard_map/ppermute | solution.py:17
  135.7 0.8 fusion.6
  137.0 2.6 collective-permute-done.3
  139.9 1.3 collective-permute-start.4
  141.2 23.9 %collective-permute-done.4 = f32[512,512]{1,0:T(8,128)S(1)} collective-permute-done((f32[512,512]{1,0:T(8,128)S(1)}, f32[512,512]{1,0:T(8,128)S(1)}, u32[]{:S(2)}, u32[]{:S(2)}) %collective-permute-start.4) | collective-permute-done | bytes 1048608 | tf_op jit(solution)/shard_map/ppermute | solution.py:17
  165.4 1.8 collective-permute-start.5
  167.2 22.6 %collective-permute-done.5 = f32[512,512]{1,0:T(8,128)S(1)} collective-permute-done((f32[512,512]{1,0:T(8,128)S(1)}, f32[512,512]{1,0:T(8,128)S(1)}, u32[]{:S(2)}, u32[]{:S(2)}) %collective-permute-start.5) | collective-permute-done | bytes 1048608 | tf_op jit(solution)/shard_map/ppermute | solution.py:17
  190.0 0.8 fusion.7
  191.4 2.6 collective-permute-done.6
  194.2 1.3 collective-permute-start.7
  195.6 23.9 %collective-permute-done.7 = f32[512,512]{1,0:T(8,128)S(1)} collective-permute-done((f32[512,512]{1,0:T(8,128)S(1)}, f32[512,512]{1,0:T(8,128)S(1)}, u32[]{:S(2)}, u32[]{:S(2)}) %collective-permute-start.7) | collective-permute-done | bytes 1048608 | tf_op jit(solution)/shard_map/ppermute | solution.py:17
  219.7 1.8 collective-permute-start.8
  221.5 22.6 %collective-permute-done.8 = f32[512,512]{1,0:T(8,128)S(1)} collective-permute-done((f32[512,512]{1,0:T(8,128)S(1)}, f32[512,512]{1,0:T(8,128)S(1)}, u32[]{:S(2)}, u32[]{:S(2)}) %collective-permute-start.8) | collective-permute-done | bytes 1048608 | tf_op jit(solution)/shard_map/ppermute | solution.py:17
  244.4 1.6 fusion.8
  245.9 4.4 %all-to-all-start.2 = ((bf16[1,16,32,512]{3,2,0,1:T(8,128)(2,1)}), bf16[1,16,32,512]{3,2,0,1:T(8,128)(2,1)S(1)}, u32[]{:S(2)}, u32[]{:S(2)}) async-start(bf16[1,16,32,512]{3,2,0,1:T(8,128)(2,1)} %bitcast.5), calls=%async_computation.2 | async-start | bytes 1048576 | tf_op jit(solution)/shard_map/all_to_all | solution.py:102
  250.4 1.3 fusion.21
  251.8 1.2 broadcast_divide_fusion
  253.0 11.6 %all-to-all-done.2 = bf16[1,16,32,512]{3,2,0,1:T(8,128)(2,1)S(1)} async-done(((bf16[1,16,32,512]{3,2,0,1:T(8,128)(2,1)}), bf16[1,16,32,512]{3,2,0,1:T(8,128)(2,1)S(1)}, u32[]{:S(2)}, u32[]{:S(2)}) %all-to-all-start.2) | async-done | bytes 524320 | tf_op jit(solution)/shard_map/all_to_all | solution.py:102
  264.6 1.1 convert_multiply_fusion
  (34 shorter events, 5.0 us)
Async XLA Ops:
  0.6 4.4 %copy-start.2 = (s32[2]{0:T(128)S(1)}, s32[2]{0:T(128)}, u32[]{:S(2)}) copy-start(s32[2]{0:T(128)} %param.6) | copy-start | bytes 28
  0.6 4.5 %copy-start = (f32[8]{0:T(128)S(1)}, f32[8]{0:T(128)}, u32[]{:S(2)}) copy-start(f32[8]{0:T(128)} %param.7) | copy-start | bytes 100
  0.7 5.1 %copy-start.1 = (s32[4]{0:T(128)S(1)}, s32[4]{0:T(128)}, u32[]{:S(2)}) copy-start(s32[4]{0:T(128)} %param.5) | copy-start | bytes 52
  0.7 18.8 %all-to-all-start = ((bf16[1,2,2,256,512]{4,3,2,0,1:T(8,128)(2,1)}), bf16[1,2,2,256,512]{4,3,2,0,1:T(8,128)(2,1)S(1)}, u32[]{:S(2)}, u32[]{:S(2)}) async-start(bf16[1,2,2,256,512]{4,3,2,0,1:T(8,128)(2,1)} %bitcast.31), calls=%async_computation | async-start | bytes 2097152 | tf_op jit(solution)/shard_map/all_to_all | solution.py:73
  82.4 2.7 %collective-permute-start = (f32[512,512]{1,0:T(8,128)S(1)}, f32[512,512]{1,0:T(8,128)S(1)}, u32[]{:S(2)}, u32[]{:S(2)}) collective-permute-start(f32[512,512]{1,0:T(8,128)S(1)} %fusion.22), channel_id=1, source_target_pairs={{0,1},{1,0},{2,3},{3,2},{4,5},{5,4},{6,7},{7,6},{8,9},{9,8},{10,11... | collective-permute-start | bytes 3145736 | tf_op jit(solution)/shard_map/ppermute | solution.py:17
  85.3 25.3 %collective-permute-start.1 = (f32[512,512]{1,0:T(8,128)S(1)}, f32[512,512]{1,0:T(8,128)S(1)}, u32[]{:S(2)}, u32[]{:S(2)}) collective-permute-start(f32[512,512]{1,0:T(8,128)S(1)} %add.76), channel_id=1, source_target_pairs={{0,2},{1,3},{2,0},{3,1},{4,6},{5,7},{6,4},{7,5},{8,10},{9,11},{10,... | collective-permute-start | bytes 3145736 | tf_op jit(solution)/shard_map/ppermute | solution.py:17
  110.8 24.7 %collective-permute-start.2 = (f32[512,512]{1,0:T(8,128)S(1)}, f32[512,512]{1,0:T(8,128)S(1)}, u32[]{:S(2)}, u32[]{:S(2)}) collective-permute-start(f32[512,512]{1,0:T(8,128)S(1)} %add.77), channel_id=1, source_target_pairs={{0,4},{1,5},{2,6},{3,7},{4,0},{5,1},{6,2},{7,3},{8,12},{9,13},{10,... | collective-permute-start | bytes 3145736 | tf_op jit(solution)/shard_map/ppermute | solution.py:17
  137.0 2.7 %collective-permute-start.3 = (f32[512,512]{1,0:T(8,128)S(1)}, f32[512,512]{1,0:T(8,128)S(1)}, u32[]{:S(2)}, u32[]{:S(2)}) collective-permute-start(f32[512,512]{1,0:T(8,128)S(1)} %fusion.23), channel_id=1, source_target_pairs={{0,1},{1,0},{2,3},{3,2},{4,5},{5,4},{6,7},{7,6},{8,9},{9,8},{10,11... | collective-permute-start | bytes 3145736 | tf_op jit(solution)/shard_map/ppermute | solution.py:17
  139.9 25.3 %collective-permute-start.4 = (f32[512,512]{1,0:T(8,128)S(1)}, f32[512,512]{1,0:T(8,128)S(1)}, u32[]{:S(2)}, u32[]{:S(2)}) collective-permute-start(f32[512,512]{1,0:T(8,128)S(1)} %add.81), channel_id=1, source_target_pairs={{0,2},{1,3},{2,0},{3,1},{4,6},{5,7},{6,4},{7,5},{8,10},{9,11},{10,... | collective-permute-start | bytes 3145736 | tf_op jit(solution)/shard_map/ppermute | solution.py:17
  165.4 24.4 %collective-permute-start.5 = (f32[512,512]{1,0:T(8,128)S(1)}, f32[512,512]{1,0:T(8,128)S(1)}, u32[]{:S(2)}, u32[]{:S(2)}) collective-permute-start(f32[512,512]{1,0:T(8,128)S(1)} %add.82), channel_id=1, source_target_pairs={{0,4},{1,5},{2,6},{3,7},{4,0},{5,1},{6,2},{7,3},{8,12},{9,13},{10,... | collective-permute-start | bytes 3145736 | tf_op jit(solution)/shard_map/ppermute | solution.py:17
  191.3 2.7 %collective-permute-start.6 = (f32[512,512]{1,0:T(8,128)S(1)}, f32[512,512]{1,0:T(8,128)S(1)}, u32[]{:S(2)}, u32[]{:S(2)}) collective-permute-start(f32[512,512]{1,0:T(8,128)S(1)} %fusion.24), channel_id=1, source_target_pairs={{0,1},{1,0},{2,3},{3,2},{4,5},{5,4},{6,7},{7,6},{8,9},{9,8},{10,11... | collective-permute-start | bytes 3145736 | tf_op jit(solution)/shard_map/ppermute | solution.py:17
  194.2 25.3 %collective-permute-start.7 = (f32[512,512]{1,0:T(8,128)S(1)}, f32[512,512]{1,0:T(8,128)S(1)}, u32[]{:S(2)}, u32[]{:S(2)}) collective-permute-start(f32[512,512]{1,0:T(8,128)S(1)} %add.86), channel_id=1, source_target_pairs={{0,2},{1,3},{2,0},{3,1},{4,6},{5,7},{6,4},{7,5},{8,10},{9,11},{10,... | collective-permute-start | bytes 3145736 | tf_op jit(solution)/shard_map/ppermute | solution.py:17
  219.7 24.4 %collective-permute-start.8 = (f32[512,512]{1,0:T(8,128)S(1)}, f32[512,512]{1,0:T(8,128)S(1)}, u32[]{:S(2)}, u32[]{:S(2)}) collective-permute-start(f32[512,512]{1,0:T(8,128)S(1)} %add.87), channel_id=1, source_target_pairs={{0,4},{1,5},{2,6},{3,7},{4,0},{5,1},{6,2},{7,3},{8,12},{9,13},{10,... | collective-permute-start | bytes 3145736 | tf_op jit(solution)/shard_map/ppermute | solution.py:17
  245.9 18.7 %all-to-all-start.2 = ((bf16[1,16,32,512]{3,2,0,1:T(8,128)(2,1)}), bf16[1,16,32,512]{3,2,0,1:T(8,128)(2,1)S(1)}, u32[]{:S(2)}, u32[]{:S(2)}) async-start(bf16[1,16,32,512]{3,2,0,1:T(8,128)(2,1)} %bitcast.5), calls=%async_computation.2 | async-start | bytes 1048576 | tf_op jit(solution)/shard_map/all_to_all | solution.py:102
where the time goes:
time: 266 us
  waiting for transfers between devices  172 us (65%)
  blocking collectives  59.3 us (22%)
  starting transfers between devices  18.3 us (7%)
  other arithmetic  9.43 us (4%)
  matrix products  4.55 us (2%)
    ppermute x9, waiting for transfers between devices, partner(): lax.ppermute(shard, axis, [(i, i ^ 1 << stride) for i in range(lax.axis_s...  148 us
    psum x1, blocking collectives, share_scores(): return lax.psum((aligned, squares, norm_slots), ('domain', 'fsdp'))  39.8 us
    all_to_all x1, blocking collectives, body(): lax.all_to_all(scaled, 'fsdp', split_axis=0, concat_axis=1, tiled=True)  19.5 us
    all_to_all x1, waiting for transfers between devices, body(): lax.all_to_all(gradients.reshape(1, groups, per_domain, rows_src, columns...  12.7 us
    all_to_all x1, waiting for transfers between devices, body(): lax.all_to_all(finished.reshape(1, shards, sub_rows, columns), 'fsdp', sp...  11.6 us
    ppermute x9, starting transfers between devices, partner(): lax.ppermute(shard, axis, [(i, i ^ 1 << stride) for i in range(lax.axis_s...  9.5 us
  transfers between devices with their start and end apart: 11, of which 11 were waited for; matrix products, arithmetic and copies ran while one was open for 2% of the time, Pallas kernels for 0%

commit v1 on v0

--- a/solution.py
+++ b/solution.py
@@ -11,6 +11,17 @@
 COEF_C = 2.0315
 MUON_SCALE = 0.2
 ETA = 4.0
+
+
+def in_blocks(x, dim, devices):
+    before, after = (x.shape[:dim], x.shape[dim + 1 :])
+    return jnp.moveaxis(x.reshape(*before, devices, -1, *after), dim, 0)
+
+
+def joined_along(tiles, dim):
+    dims = list(tiles.shape[1:])
+    dims[dim] *= tiles.shape[0]
+    return jnp.moveaxis(tiles, 0, dim).reshape(dims)
 
 
 def partner(shard, axis, stride):
@@ -99,13 +110,15 @@
     start_rows = lax.all_to_all(scaled, "fsdp", split_axis=0, concat_axis=1, tiled=True)
     start_rows = lax.optimization_barrier(start_rows.reshape(own_rows, columns))
     finished = newton_steps(start_rows)
-    returned = lax.all_to_all(
-        finished.reshape(1, shards, sub_rows, columns),
-        "fsdp",
-        split_axis=1,
-        concat_axis=0,
-        tiled=True,
-    )
+    x = finished.reshape(1, shards, sub_rows, columns)
+    size, index = (lax.axis_size("fsdp"), lax.axis_index("fsdp"))
+    tiles = in_blocks(x, 1, size)
+    outs = [tiles[index]]
+    for turn in range(1, size):
+        sent = tiles[(index + turn) % size]
+        outs.append(lax.ppermute(sent, "fsdp", [(i_2, (i_2 + turn) % size) for i_2 in range(size)]))
+    tiles = jnp.stack(outs)[(index - jnp.arange(size)) % size]
+    returned = joined_along(tiles, 0)
     returned = returned.reshape(per_domain, rows_src, columns)
     updates = returned.astype(jnp.float32) * (MUON_SCALE * math.sqrt(full_rows))
     total_sq = jnp.sum(norm_slots)

time: 266 us -> 272 us (1.023)
  starting transfers between devices: 18.3 us -> 35.4 us
  waiting for transfers between devices: 172 us -> 162 us
    ppermute x0 -> x15, starting transfers between devices: none -> 21.5 us  [body(): lax.ppermute(sent, 'fsdp', [(i_2, (i_2 + turn) % size) for i_2 in range(s...]
    all_to_all x1 -> x0, waiting for transfers between devices: 11.6 us -> none  [body(): lax.all_to_all(finished.reshape(1, shards, sub_rows, columns), 'fsdp', sp...]
    all_to_all x1 -> x0, starting transfers between devices: 4.4 us -> none  [body(): lax.all_to_all(finished.reshape(1, shards, sub_rows, columns), 'fsdp', sp...]
  transfers between devices with their start and end apart: 11 -> 25, of which waited for: 11 -> 12; matrix products, arithmetic and copies ran while one was open for 2% -> 2% of each run, Pallas kernels for 0% -> 0%
where the time goes in v1:
time: 272 us
  waiting for transfers between devices  162 us (60%)
  blocking collectives  59.3 us (22%)
  starting transfers between devices  35.4 us (13%)
  other arithmetic  9.32 us (3%)
  matrix products  3.76 us (1%)
    ppermute x9, waiting for transfers between devices, partner(): lax.ppermute(shard, axis, [(i, i ^ 1 << stride) for i in range(lax.axis_s...  147 us
    psum x1, blocking collectives, share_scores(): return lax.psum((aligned, squares, norm_slots), ('domain', 'fsdp'))  39.8 us
    ppermute x15, starting transfers between devices, body(): lax.ppermute(sent, 'fsdp', [(i_2, (i_2 + turn) % size) for i_2 in range(s...  21.5 us
    all_to_all x1, blocking collectives, body(): lax.all_to_all(scaled, 'fsdp', split_axis=0, concat_axis=1, tiled=True)  19.5 us
    all_to_all x1, waiting for transfers between devices, body(): lax.all_to_all(gradients.reshape(1, groups, per_domain, rows_src, columns...  12.7 us
    ppermute x9, starting transfers between devices, partner(): lax.ppermute(shard, axis, [(i, i ^ 1 << stride) for i in range(lax.axis_s...  9.47 us
  transfers between devices with their start and end apart: 25, of which 12 were waited for; matrix products, arithmetic and copies ran while one was open for 2% of the time, Pallas kernels for 0%

profile of v1, /device:TPU:0, one launch (start us, length us, event | category | flops | bytes accessed | tf_op | source)
XLA Modules:
  0.0 272.1 jit_solution(4355042236437863641)
XLA Ops:
  0.7 4.4 %all-to-all-start = ((bf16[1,2,2,256,512]{4,3,2,0,1:T(8,128)(2,1)}), bf16[1,2,2,256,512]{4,3,2,0,1:T(8,128)(2,1)S(1)}, u32[]{:S(2)}, u32[]{:S(2)}) async-start(bf16[1,2,2,256,512]{4,3,2,0,1:T(8,128)(2,1)} %bitcast.92), calls=%async_computation | async-start | bytes 2097152 | tf_op jit(solution)/shard_map/all_to_all | solution.py:84
  6.7 12.7 %all-to-all-done = bf16[1,2,2,256,512]{4,3,2,0,1:T(8,128)(2,1)S(1)} async-done(((bf16[1,2,2,256,512]{4,3,2,0,1:T(8,128)(2,1)}), bf16[1,2,2,256,512]{4,3,2,0,1:T(8,128)(2,1)S(1)}, u32[]{:S(2)}, u32[]{:S(2)}) %all-to-all-start) | async-done | bytes 1048608 | tf_op jit(solution)/shard_map/all_to_all | solution.py:84
  20.9 39.8 %all-reduce = (f32[4]{0:T(128)S(1)}, f32[2]{0:T(128)S(1)}, f32[2]{0:T(128)S(1)}) all-reduce(f32[4]{0:T(128)S(1)} %dynamic_update_slice.3, f32[2]{0:T(128)S(1)} %get-tuple-element.3, f32[2]{0:T(128)S(1)} %get-tuple-element.2), channel_id=1, replica_groups=mesh['domain'=2,'fsdp'=16] {'domain','fsdp'}, use_global_device_ids=true, to_apply=%region_5.6 | all-reduce | flops 8 | bytes 64 | tf_op jit(solution)/shard_map/psum | solution.py:66
  62.4 19.5 %all_to_all.8 = bf16[16,1,32,512]{3,2,1,0:T(8,128)(2,1)S(1)} all-to-all(bf16[16,1,32,512]{3,2,1,0:T(8,128)(2,1)S(1)} %divide_convert_fusion), channel_id=1, replica_groups=mesh['domain'=2,'fsdp'=16] {'fsdp'}, dimensions={0} | all-to-all | bytes 1048576 | tf_op jit(solution)/shard_map/all_to_all | solution.py:110
  82.6 2.5 collective-permute-done
  85.3 1.1 collective-permute-start.1
  86.4 24.2 %collective-permute-done.1 = f32[512,512]{1,0:T(8,128)S(1)} collective-permute-done((f32[512,512]{1,0:T(8,128)S(1)}, f32[512,512]{1,0:T(8,128)S(1)}, u32[]{:S(2)}, u32[]{:S(2)}) %collective-permute-start.1) | collective-permute-done | bytes 1048608 | tf_op jit(solution)/shard_map/ppermute | solution.py:28
  110.8 1.8 collective-permute-start.2
  112.6 22.8 %collective-permute-done.2 = f32[512,512]{1,0:T(8,128)S(1)} collective-permute-done((f32[512,512]{1,0:T(8,128)S(1)}, f32[512,512]{1,0:T(8,128)S(1)}, u32[]{:S(2)}, u32[]{:S(2)}) %collective-permute-start.2) | collective-permute-done | bytes 1048608 | tf_op jit(solution)/shard_map/ppermute | solution.py:28
  137.0 2.6 collective-permute-done.3
  139.9 1.3 collective-permute-start.4
  141.2 24.0 %collective-permute-done.4 = f32[512,512]{1,0:T(8,128)S(1)} collective-permute-done((f32[512,512]{1,0:T(8,128)S(1)}, f32[512,512]{1,0:T(8,128)S(1)}, u32[]{:S(2)}, u32[]{:S(2)}) %collective-permute-start.4) | collective-permute-done | bytes 1048608 | tf_op jit(solution)/shard_map/ppermute | solution.py:28
  165.4 1.8 collective-permute-start.5
  167.2 22.6 %collective-permute-done.5 = f32[512,512]{1,0:T(8,128)S(1)} collective-permute-done((f32[512,512]{1,0:T(8,128)S(1)}, f32[512,512]{1,0:T(8,128)S(1)}, u32[]{:S(2)}, u32[]{:S(2)}) %collective-permute-start.5) | collective-permute-done | bytes 1048608 | tf_op jit(solution)/shard_map/ppermute | solution.py:28
  191.4 2.6 collective-permute-done.6
  194.2 1.3 collective-permute-start.7
  195.5 24.0 %collective-permute-done.7 = f32[512,512]{1,0:T(8,128)S(1)} collective-permute-done((f32[512,512]{1,0:T(8,128)S(1)}, f32[512,512]{1,0:T(8,128)S(1)}, u32[]{:S(2)}, u32[]{:S(2)}) %collective-permute-start.7) | collective-permute-done | bytes 1048608 | tf_op jit(solution)/shard_map/ppermute | solution.py:28
  219.7 1.8 collective-permute-start.8
  221.6 1.3 fusion.23
  222.9 21.2 %collective-permute-done.8 = f32[512,512]{1,0:T(8,128)S(1)} collective-permute-done((f32[512,512]{1,0:T(8,128)S(1)}, f32[512,512]{1,0:T(8,128)S(1)}, u32[]{:S(2)}, u32[]{:S(2)}) %collective-permute-start.8) | collective-permute-done | bytes 1048608 | tf_op jit(solution)/shard_map/ppermute | solution.py:28
  245.3 1.2 broadcast_divide_fusion
  246.5 1.2 collective-permute-start.10
  247.8 2.3 collective-permute-start.11
  251.4 2.2 collective-permute-start.14
  253.5 2.6 collective-permute-start.15
  256.2 2.1 collective-permute-start.16
  258.3 1.2 collective-permute-start.18
  259.5 4.0 %collective-permute-start.19 = (bf16[1,1,32,512]{3,2,1,0:T(8,128)(2,1)S(1)}, bf16[1,1,32,512]{3,2,1,0:T(8,128)(2,1)S(1)}, u32[]{:S(2)}, u32[]{:S(2)}) collective-permute-start(bf16[1,1,32,512]{3,2,1,0:T(8,128)(2,1)S(1)} %get-tuple-element.13), channel_id=1, source_target_pairs={{0,11},{1,12},{2,13},{3,14},{4,15},{5,0},{6,1},{7,2},{8,3},{9,4},{... | collective-permute-start | bytes 98312 | tf_op jit(solution)/shard_map/ppermute | solution.py:119
  264.2 2.5 collective-permute-start.22
  266.8 2.0 collective-permute-start.23
  268.8 1.5 collective-permute-done.23
  270.9 1.1 convert_multiply_fusion
  (81 shorter events, 13.3 us)
Async XLA Ops:
  0.6 4.4 %copy-start.2 = (s32[2]{0:T(128)S(1)}, s32[2]{0:T(128)}, u32[]{:S(2)}) copy-start(s32[2]{0:T(128)} %param.6) | copy-start | bytes 28
  0.6 4.5 %copy-start.1 = (s32[4]{0:T(128)S(1)}, s32[4]{0:T(128)}, u32[]{:S(2)}) copy-start(s32[4]{0:T(128)} %param.5) | copy-start | bytes 52
  0.7 4.6 %copy-start = (f32[8]{0:T(128)S(1)}, f32[8]{0:T(128)}, u32[]{:S(2)}) copy-start(f32[8]{0:T(128)} %param.7) | copy-start | bytes 100
  0.7 18.8 %all-to-all-start = ((bf16[1,2,2,256,512]{4,3,2,0,1:T(8,128)(2,1)}), bf16[1,2,2,256,512]{4,3,2,0,1:T(8,128)(2,1)S(1)}, u32[]{:S(2)}, u32[]{:S(2)}) async-start(bf16[1,2,2,256,512]{4,3,2,0,1:T(8,128)(2,1)} %bitcast.92), calls=%async_computation | async-start | bytes 2097152 | tf_op jit(solution)/shard_map/all_to_all | solution.py:84
  82.3 2.7 %collective-permute-start = (f32[512,512]{1,0:T(8,128)S(1)}, f32[512,512]{1,0:T(8,128)S(1)}, u32[]{:S(2)}, u32[]{:S(2)}) collective-permute-start(f32[512,512]{1,0:T(8,128)S(1)} %fusion.24), channel_id=1, source_target_pairs={{0,1},{1,0},{2,3},{3,2},{4,5},{5,4},{6,7},{7,6},{8,9},{9,8},{10,11... | collective-permute-start | bytes 3145736 | tf_op jit(solution)/shard_map/ppermute | solution.py:28
  85.3 25.3 %collective-permute-start.1 = (f32[512,512]{1,0:T(8,128)S(1)}, f32[512,512]{1,0:T(8,128)S(1)}, u32[]{:S(2)}, u32[]{:S(2)}) collective-permute-start(f32[512,512]{1,0:T(8,128)S(1)} %add.238), channel_id=1, source_target_pairs={{0,2},{1,3},{2,0},{3,1},{4,6},{5,7},{6,4},{7,5},{8,10},{9,11},{10,... | collective-permute-start | bytes 3145736 | tf_op jit(solution)/shard_map/ppermute | solution.py:28
  110.8 24.7 %collective-permute-start.2 = (f32[512,512]{1,0:T(8,128)S(1)}, f32[512,512]{1,0:T(8,128)S(1)}, u32[]{:S(2)}, u32[]{:S(2)}) collective-permute-start(f32[512,512]{1,0:T(8,128)S(1)} %add.239), channel_id=1, source_target_pairs={{0,4},{1,5},{2,6},{3,7},{4,0},{5,1},{6,2},{7,3},{8,12},{9,13},{10,... | collective-permute-start | bytes 3145736 | tf_op jit(solution)/shard_map/ppermute | solution.py:28
  137.0 2.7 %collective-permute-start.3 = (f32[512,512]{1,0:T(8,128)S(1)}, f32[512,512]{1,0:T(8,128)S(1)}, u32[]{:S(2)}, u32[]{:S(2)}) collective-permute-start(f32[512,512]{1,0:T(8,128)S(1)} %fusion.25), channel_id=1, source_target_pairs={{0,1},{1,0},{2,3},{3,2},{4,5},{5,4},{6,7},{7,6},{8,9},{9,8},{10,11... | collective-permute-start | bytes 3145736 | tf_op jit(solution)/shard_map/ppermute | solution.py:28
  139.9 25.3 %collective-permute-start.4 = (f32[512,512]{1,0:T(8,128)S(1)}, f32[512,512]{1,0:T(8,128)S(1)}, u32[]{:S(2)}, u32[]{:S(2)}) collective-permute-start(f32[512,512]{1,0:T(8,128)S(1)} %add.243), channel_id=1, source_target_pairs={{0,2},{1,3},{2,0},{3,1},{4,6},{5,7},{6,4},{7,5},{8,10},{9,11},{10,... | collective-permute-start | bytes 3145736 | tf_op jit(solution)/shard_map/ppermute | solution.py:28
  165.4 24.4 %collective-permute-start.5 = (f32[512,512]{1,0:T(8,128)S(1)}, f32[512,512]{1,0:T(8,128)S(1)}, u32[]{:S(2)}, u32[]{:S(2)}) collective-permute-start(f32[512,512]{1,0:T(8,128)S(1)} %add.244), channel_id=1, source_target_pairs={{0,4},{1,5},{2,6},{3,7},{4,0},{5,1},{6,2},{7,3},{8,12},{9,13},{10,... | collective-permute-start | bytes 3145736 | tf_op jit(solution)/shard_map/ppermute | solution.py:28
  191.3 2.7 %collective-permute-start.6 = (f32[512,512]{1,0:T(8,128)S(1)}, f32[512,512]{1,0:T(8,128)S(1)}, u32[]{:S(2)}, u32[]{:S(2)}) collective-permute-start(f32[512,512]{1,0:T(8,128)S(1)} %fusion.26), channel_id=1, source_target_pairs={{0,1},{1,0},{2,3},{3,2},{4,5},{5,4},{6,7},{7,6},{8,9},{9,8},{10,11... | collective-permute-start | bytes 3145736 | tf_op jit(solution)/shard_map/ppermute | solution.py:28
  194.2 25.3 %collective-permute-start.7 = (f32[512,512]{1,0:T(8,128)S(1)}, f32[512,512]{1,0:T(8,128)S(1)}, u32[]{:S(2)}, u32[]{:S(2)}) collective-permute-start(f32[512,512]{1,0:T(8,128)S(1)} %add.248), channel_id=1, source_target_pairs={{0,2},{1,3},{2,0},{3,1},{4,6},{5,7},{6,4},{7,5},{8,10},{9,11},{10,... | collective-permute-start | bytes 3145736 | tf_op jit(solution)/shard_map/ppermute | solution.py:28
  219.7 24.4 %collective-permute-start.8 = (f32[512,512]{1,0:T(8,128)S(1)}, f32[512,512]{1,0:T(8,128)S(1)}, u32[]{:S(2)}, u32[]{:S(2)}) collective-permute-start(f32[512,512]{1,0:T(8,128)S(1)} %add.249), channel_id=1, source_target_pairs={{0,4},{1,5},{2,6},{3,7},{4,0},{5,1},{6,2},{7,3},{8,12},{9,13},{10,... | collective-permute-start | bytes 3145736 | tf_op jit(solution)/shard_map/ppermute | solution.py:28
  245.3 6.1 %collective-permute-start.9 = (bf16[1,1,32,512]{3,2,1,0:T(8,128)(2,1)S(1)}, bf16[1,1,32,512]{3,2,1,0:T(8,128)(2,1)S(1)}, u32[]{:S(2)}, u32[]{:S(2)}) collective-permute-start(bf16[1,1,32,512]{3,2,1,0:T(8,128)(2,1)S(1)} %get-tuple-element.23), channel_id=1, source_target_pairs={{0,1},{1,2},{2,3},{3,4},{4,5},{5,6},{6,7},{7,8},{8,9},{9,10},{10,1... | collective-permute-start | bytes 98312 | tf_op jit(solution)/shard_map/ppermute | solution.py:119
  246.5 7.0 %collective-permute-start.10 = (bf16[1,1,32,512]{3,2,1,0:T(8,128)(2,1)S(1)}, bf16[1,1,32,512]{3,2,1,0:T(8,128)(2,1)S(1)}, u32[]{:S(2)}, u32[]{:S(2)}) collective-permute-start(bf16[1,1,32,512]{3,2,1,0:T(8,128)(2,1)S(1)} %get-tuple-element.22), channel_id=1, source_target_pairs={{0,2},{1,3},{2,4},{3,5},{4,6},{5,7},{6,8},{7,9},{8,10},{9,11},{10,... | collective-permute-start | bytes 98312 | tf_op jit(solution)/shard_map/ppermute | solution.py:119
  247.8 8.4 %collective-permute-start.11 = (bf16[1,1,32,512]{3,2,1,0:T(8,128)(2,1)S(1)}, bf16[1,1,32,512]{3,2,1,0:T(8,128)(2,1)S(1)}, u32[]{:S(2)}, u32[]{:S(2)}) collective-permute-start(bf16[1,1,32,512]{3,2,1,0:T(8,128)(2,1)S(1)} %get-tuple-element.21), channel_id=1, source_target_pairs={{0,3},{1,4},{2,5},{3,6},{4,7},{5,8},{6,9},{7,10},{8,11},{9,12},{10... | collective-permute-start | bytes 98312 | tf_op jit(solution)/shard_map/ppermute | solution.py:119
  250.0 8.2 %collective-permute-start.12 = (bf16[1,1,32,512]{3,2,1,0:T(8,128)(2,1)S(1)}, bf16[1,1,32,512]{3,2,1,0:T(8,128)(2,1)S(1)}, u32[]{:S(2)}, u32[]{:S(2)}) collective-permute-start(bf16[1,1,32,512]{3,2,1,0:T(8,128)(2,1)S(1)} %get-tuple-element.20), channel_id=1, source_target_pairs={{0,4},{1,5},{2,6},{3,7},{4,8},{5,9},{6,10},{7,11},{8,12},{9,13},{1... | collective-permute-start | bytes 98312 | tf_op jit(solution)/shard_map/ppermute | solution.py:119
  250.7 7.6 %collective-permute-start.13 = (bf16[1,1,32,512]{3,2,1,0:T(8,128)(2,1)S(1)}, bf16[1,1,32,512]{3,2,1,0:T(8,128)(2,1)S(1)}, u32[]{:S(2)}, u32[]{:S(2)}) collective-permute-start(bf16[1,1,32,512]{3,2,1,0:T(8,128)(2,1)S(1)} %get-tuple-element.19), channel_id=1, source_target_pairs={{0,5},{1,6},{2,7},{3,8},{4,9},{5,10},{6,11},{7,12},{8,13},{9,14},{... | collective-permute-start | bytes 98312 | tf_op jit(solution)/shard_map/ppermute | solution.py:119
  251.4 8.1 %collective-permute-start.14 = (bf16[1,1,32,512]{3,2,1,0:T(8,128)(2,1)S(1)}, bf16[1,1,32,512]{3,2,1,0:T(8,128)(2,1)S(1)}, u32[]{:S(2)}, u32[]{:S(2)}) collective-permute-start(bf16[1,1,32,512]{3,2,1,0:T(8,128)(2,1)S(1)} %get-tuple-element.18), channel_id=1, source_target_pairs={{0,6},{1,7},{2,8},{3,9},{4,10},{5,11},{6,12},{7,13},{8,14},{9,15},... | collective-permute-start | bytes 98312 | tf_op jit(solution)/shard_map/ppermute | solution.py:119
  253.5 9.9 %collective-permute-start.15 = (bf16[1,1,32,512]{3,2,1,0:T(8,128)(2,1)S(1)}, bf16[1,1,32,512]{3,2,1,0:T(8,128)(2,1)S(1)}, u32[]{:S(2)}, u32[]{:S(2)}) collective-permute-start(bf16[1,1,32,512]{3,2,1,0:T(8,128)(2,1)S(1)} %get-tuple-element.17), channel_id=1, source_target_pairs={{0,7},{1,8},{2,9},{3,10},{4,11},{5,12},{6,13},{7,14},{8,15},{9,0},... | collective-permute-start | bytes 98312 | tf_op jit(solution)/shard_map/ppermute | solution.py:119
  256.2 7.8 %collective-permute-start.16 = (bf16[1,1,32,512]{3,2,1,0:T(8,128)(2,1)S(1)}, bf16[1,1,32,512]{3,2,1,0:T(8,128)(2,1)S(1)}, u32[]{:S(2)}, u32[]{:S(2)}) collective-permute-start(bf16[1,1,32,512]{3,2,1,0:T(8,128)(2,1)S(1)} %get-tuple-element.16), channel_id=1, source_target_pairs={{0,8},{1,9},{2,10},{3,11},{4,12},{5,13},{6,14},{7,15},{8,0},{9,1},... | collective-permute-start | bytes 98312 | tf_op jit(solution)/shard_map/ppermute | solution.py:119
  258.3 6.0 %collective-permute-start.17 = (bf16[1,1,32,512]{3,2,1,0:T(8,128)(2,1)S(1)}, bf16[1,1,32,512]{3,2,1,0:T(8,128)(2,1)S(1)}, u32[]{:S(2)}, u32[]{:S(2)}) collective-permute-start(bf16[1,1,32,512]{3,2,1,0:T(8,128)(2,1)S(1)} %get-tuple-element.15), channel_id=1, source_target_pairs={{0,9},{1,10},{2,11},{3,12},{4,13},{5,14},{6,15},{7,0},{8,1},{9,2},... | collective-permute-start | bytes 98312 | tf_op jit(solution)/shard_map/ppermute | solution.py:119
  258.3 8.5 %collective-permute-start.18 = (bf16[1,1,32,512]{3,2,1,0:T(8,128)(2,1)S(1)}, bf16[1,1,32,512]{3,2,1,0:T(8,128)(2,1)S(1)}, u32[]{:S(2)}, u32[]{:S(2)}) collective-permute-start(bf16[1,1,32,512]{3,2,1,0:T(8,128)(2,1)S(1)} %get-tuple-element.14), channel_id=1, source_target_pairs={{0,10},{1,11},{2,12},{3,13},{4,14},{5,15},{6,0},{7,1},{8,2},{9,3},... | collective-permute-start | bytes 98312 | tf_op jit(solution)/shard_map/ppermute | solution.py:119
  259.5 9.3 %collective-permute-start.19 = (bf16[1,1,32,512]{3,2,1,0:T(8,128)(2,1)S(1)}, bf16[1,1,32,512]{3,2,1,0:T(8,128)(2,1)S(1)}, u32[]{:S(2)}, u32[]{:S(2)}) collective-permute-start(bf16[1,1,32,512]{3,2,1,0:T(8,128)(2,1)S(1)} %get-tuple-element.13), channel_id=1, source_target_pairs={{0,11},{1,12},{2,13},{3,14},{4,15},{5,0},{6,1},{7,2},{8,3},{9,4},{... | collective-permute-start | bytes 98312 | tf_op jit(solution)/shard_map/ppermute | solution.py:119
  263.4 5.3 %collective-permute-start.20 = (bf16[1,1,32,512]{3,2,1,0:T(8,128)(2,1)S(1)}, bf16[1,1,32,512]{3,2,1,0:T(8,128)(2,1)S(1)}, u32[]{:S(2)}, u32[]{:S(2)}) collective-permute-start(bf16[1,1,32,512]{3,2,1,0:T(8,128)(2,1)S(1)} %get-tuple-element.12), channel_id=1, source_target_pairs={{0,12},{1,13},{2,14},{3,15},{4,0},{5,1},{6,2},{7,3},{8,4},{9,5},{1... | collective-permute-start | bytes 98312 | tf_op jit(solution)/shard_map/ppermute | solution.py:119
  264.0 4.8 %collective-permute-start.21 = (bf16[1,1,32,512]{3,2,1,0:T(8,128)(2,1)S(1)}, bf16[1,1,32,512]{3,2,1,0:T(8,128)(2,1)S(1)}, u32[]{:S(2)}, u32[]{:S(2)}) collective-permute-start(bf16[1,1,32,512]{3,2,1,0:T(8,128)(2,1)S(1)} %get-tuple-element.11), channel_id=1, source_target_pairs={{0,13},{1,14},{2,15},{3,0},{4,1},{5,2},{6,3},{7,4},{8,5},{9,6},{10... | collective-permute-start | bytes 98312 | tf_op jit(solution)/shard_map/ppermute | solution.py:119
  264.2 4.6 %collective-permute-start.22 = (bf16[1,1,32,512]{3,2,1,0:T(8,128)(2,1)S(1)}, bf16[1,1,32,512]{3,2,1,0:T(8,128)(2,1)S(1)}, u32[]{:S(2)}, u32[]{:S(2)}) collective-permute-start(bf16[1,1,32,512]{3,2,1,0:T(8,128)(2,1)S(1)} %get-tuple-element.10), channel_id=1, source_target_pairs={{0,14},{1,15},{2,0},{3,1},{4,2},{5,3},{6,4},{7,5},{8,6},{9,7},{10,... | collective-permute-start | bytes 98312 | tf_op jit(solution)/shard_map/ppermute | solution.py:119
  266.8 3.6 %collective-permute-start.23 = (bf16[1,1,32,512]{3,2,1,0:T(8,128)(2,1)S(1)}, bf16[1,1,32,512]{3,2,1,0:T(8,128)(2,1)S(1)}, u32[]{:S(2)}, u32[]{:S(2)}) collective-permute-start(bf16[1,1,32,512]{3,2,1,0:T(8,128)(2,1)S(1)} %get-tuple-element.9), channel_id=1, source_target_pairs={{0,15},{1,0},{2,1},{3,2},{4,3},{5,4},{6,5},{7,6},{8,7},{9,8},{10,9... | collective-permute-start | bytes 98312 | tf_op jit(solution)/shard_map/ppermute | solution.py:119
